TPU v7x, 32 devices: a whole 2x2x4 slice. The times are simulated.
32 devices in a mesh: ctx: 16 (over z, x, core), head: 2 (over y).
Axes of the slice: x: 2, y: 2, z: 4, core: 2. Of those that a mesh axis runs over, the one named last changes fastest.
Arguments:
- queries: bfloat16 [4096, 4096], P('ctx', 'head')
- keys: bfloat16 [4096, 1024], P(('ctx', 'head'))
- values: bfloat16 [4096, 1024], P(('ctx', 'head')), may hold values from -6 to 6
- selected: int32 [32, 8, 3], P('ctx', 'head'), may hold values from 0 to 6, as said below
Outputs:
- attended: bfloat16 [4096, 4096], P('ctx', 'head')
Inputs may be any that keep to these rules, and one draw needn't show every extreme that they name: selected[t, g, :] names 3 different blocks of 512 positions that lie before the block of tile t; where fewer than 3 such blocks exist, the remaining entries equal the tile's own block and name nothing more.
All inputs are finite; a program needn't handle non-finite values.
Results may differ from a plain program's by a relative error of at most 0.0041.
Values may be sent and summed in bfloat16 or wider, within the bound.
No kernel may reach another device: no remote copies, remote signals or barrier semaphores. Data moves between devices by JAX's collectives and lax.ppermute only.
A program may use at most 64 MiB of HBM per device.

v0:
```python
import math
import jax
import jax.numpy as jnp
from jax import lax
from jax.sharding import PartitionSpec as P

HD = 128
QH = 32
KVH = 8
BLK = 512
TILE = 128
floor_value = -1e30


def body(queries, keys, values, selected):
    local_rows = queries.shape[0]
    group_count = KVH // lax.axis_size("head")
    per_group = QH // KVH
    score_scale = HD ** (-0.5)
    own_keys, own_values = (
        lax.all_to_all(keys, "head", split_axis=1, concat_axis=0, tiled=True),
        lax.all_to_all(values, "head", split_axis=1, concat_axis=0, tiled=True),
    )
    query_four = queries.reshape(local_rows, group_count, per_group, HD)
    offset = lax.axis_index("ctx") * local_rows
    query_pos = offset + jnp.arange(local_rows, dtype=jnp.int32)
    query_block = query_pos // BLK
    row_select = jnp.repeat(selected, TILE, axis=0)

    def attend(running, key_rows, value_rows, first_row):
        row_count = key_rows.shape[0]
        key_pos = first_row + jnp.arange(row_count, dtype=jnp.int32)
        key_block = key_pos // BLK
        own_part = (key_block[None, :] == query_block[:, None]) & (
            key_pos[None, :] <= query_pos[:, None]
        )
        picked = jnp.any(row_select[:, :, :, None] == key_block[None, None, None, :], axis=2)
        picked = picked & (key_block[None, None, :] != query_block[:, None, None])
        allowed = jnp.transpose(picked | own_part[:, None, :], (1, 0, 2))

        def compute(current):
            running_max, totals, accumulated = current
            scores = (
                jnp.einsum(
                    "qgjd,kgd->gjqk",
                    query_four,
                    key_rows.reshape(row_count, group_count, HD),
                    preferred_element_type=jnp.float32,
                )
                * score_scale
            )
            live_mask = allowed[:, None]
            row_top = jnp.max(jnp.where(live_mask, scores, floor_value), axis=-1)
            newest = jnp.maximum(running_max, row_top)
            weights = jnp.where(live_mask, jnp.exp(scores - newest[..., None]), 0.0)
            factor = jnp.exp(running_max - newest)
            totals = totals * factor + jnp.sum(weights, axis=-1)
            product = jnp.einsum(
                "gjqk,kgd->gjqd",
                weights.astype(jnp.bfloat16),
                value_rows.reshape(row_count, group_count, HD),
                preferred_element_type=jnp.float32,
            )
            accumulated = accumulated * factor[..., None] + product
            return (newest, totals, accumulated)

        def keep_running(current):
            return current

        needed = jnp.any(allowed)
        return lax.cond(needed, compute, keep_running, running)

    start_max = jnp.full((group_count, per_group, local_rows), floor_value, jnp.float32)
    start_totals = jnp.zeros((group_count, per_group, local_rows), jnp.float32)
    start_accumulated = jnp.zeros((group_count, per_group, local_rows, HD), jnp.float32)
    key_piece = lax.all_gather(own_keys, "ctx", axis=0, tiled=True)
    value_piece = lax.all_gather(own_values, "ctx", axis=0, tiled=True)
    row_count = key_piece.shape[0]
    step_rows = math.gcd(row_count, 512)

    def loop_body(block_index, current):
        key_part = lax.dynamic_slice_in_dim(key_piece, block_index * step_rows, step_rows, 0)
        value_part = lax.dynamic_slice_in_dim(value_piece, block_index * step_rows, step_rows, 0)
        return attend(current, key_part, value_part, block_index * step_rows)

    running_max, totals, accumulated = lax.fori_loop(
        0, row_count // step_rows, loop_body, (start_max, start_totals, start_accumulated)
    )
    mixed = accumulated / totals[..., None]
    return (
        jnp.transpose(mixed, (2, 0, 1, 3))
        .reshape(local_rows, group_count * per_group * HD)
        .astype(jnp.bfloat16)
    )


def solution(mesh):
    placed = (
        P("ctx", "head"),
        P(("ctx", "head"), None),
        P(("ctx", "head"), None),
        P("ctx", "head", None),
    )
    return jax.shard_map(
        body, mesh=mesh, in_specs=placed, out_specs=P("ctx", "head"), check_vma=False
    )
```

profile of v0, /device:TPU:27, one launch (start us, length us, event | category | flops | bytes accessed | tf_op | source)
XLA Modules:
  0.0 254.5 jit_solution(11256422979810992226)
XLA Ops:
  7.8 6.7 %all_to_all.38 = bf16[128,2,512]{0,2,1:T(8,128)(2,1)S(1)} all-to-all(bf16[128,2,512]{0,2,1:T(8,128)(2,1)S(1)} %bitcast.60), channel_id=1, replica_groups=mesh['ctx'=16,'head'=2] {'head'}, dimensions={1} | all-to-all | bytes 524288 | tf_op jit(solution)/shard_map/all_to_all | solution.py:21
  16.5 6.4 %all_to_all.39 = bf16[128,2,512]{0,2,1:T(8,128)(2,1)S(1)} all-to-all(bf16[128,2,512]{0,2,1:T(8,128)(2,1)S(1)} %bitcast.61), channel_id=1, replica_groups=mesh['ctx'=16,'head'=2] {'head'}, dimensions={1} | all-to-all | bytes 524288 | tf_op jit(solution)/shard_map/all_to_all | solution.py:22
  25.8 39.4 %all-gather.3.cloned.1.call-done = bf16[4096,512]{1,0:T(8,128)(2,1)} async-done(((bf16[256,512]{1,0:T(8,128)(2,1)}), bf16[4096,512]{1,0:T(8,128)(2,1)}) %all-gather.3.cloned.1.call-update) | async-done | bytes 4194320 | tf_op jit(solution)/shard_map/all_gather | solution.py:76
  65.2 6.4 %copy.69 = bf16[4096,512]{0,1:T(8,128)(2,1)} copy(bf16[4096,512]{1,0:T(8,128)(2,1)} %all-gather.3.cloned.1.call-done) | data formatting | bytes 8388608
  71.6 44.8 %all-gather.5.cloned.1.call-done = bf16[4096,512]{1,0:T(8,128)(2,1)} async-done(((bf16[256,512]{1,0:T(8,128)(2,1)}), bf16[4096,512]{1,0:T(8,128)(2,1)}) %all-gather.5.cloned.1.call-update) | async-done | bytes 4194320 | tf_op jit(solution)/shard_map/all_gather | solution.py:77
  116.4 6.5 %copy.71 = bf16[4096,512]{0,1:T(8,128)(2,1)} copy(bf16[4096,512]{1,0:T(8,128)(2,1)} %all-gather.5.cloned.1.call-done) | data formatting | bytes 8388608
  122.9 1.6 broadcast_in_dim.69
  124.5 118.8 %while.21 = (s32[]{:T(128)}, f32[4,4,256]{2,1,0:T(4,128)S(1)}, f32[4,4,256]{2,1,0:T(4,128)S(1)}, f32[4,4,256,128]{3,2,1,0:T(8,128)}, bf16[4096,512]{0,1:T(8,128)...) while((s32[]{:T(128)}, f32[4,4,256]{2,1,0:T(4,128)S(1)}, ...), condition=%wide.region_7.8_spmd.clone.clone, body=%wide.region_0.7_spmd.clone.clone.sunk | while | flops 1103646720 | bytes 56711624 | solution.py:86
  128.2 11.1 %conditional.4 = ((f32[4,4,256]{2,1,0:T(4,128)S(1)}, f32[4,4,256]{2,1,0:T(4,128)S(1)}, f32[4,4,256,128]{3,2,1,0:T(8,128)})) conditional(s32[]{:T(128)} %convert_element_type.38, (f32[4,4,256]{2,1,0:T(4,128)S(1)}, f32[4,4,256]{2,1,0:T(4,128)S(1)}, f32[4,4,256,128]{3,2,1,0:T(8,128)}) %tuple.84, (pred[256,512]{0,1:T(8,128)(4,1)S(1)}, ...), branch_computations={%region_3.3_spmd, %region_4.6_spmd} | conditional | flops 1098915840 | bytes 54526076 | solution.py:71
  130.9 1.9 fusion.6
  132.8 1.8 fusion.10
  134.6 3.3 %multiply_add_fusion = f32[4,4,256,128]{3,2,1,0:T(8,128)S(1)} fusion(f32[4,4,256,128]{3,2,1,0:T(8,128)S(1)} %copy-done, bf16[512,4,128,1]{0,2,3,1:T(8,128)(2,1)S(1)} %bitcast.53, f32[4,512,256,4]{2,1,3,0:T(8,128)S(1)} %get-tuple-element.534, f32[4,4,256]{2,1,0:T(4,128)S(1)} %max.5, pred[4,256,512]{1,2,0:T(8,128)(4,1)S(1)} %and_or_fusion, ...), kind=kOutput, calls=%fused_computation.15 | convolution fusion | flops 546308096 | bytes 13664256 | tf_op jit(solution)/shard_map/while/body/eval_jaxpr/cond/branch_1_fun/gjqk,kgd->gjqd/dot_general | solution.py:58
  138.0 1.3 copy-done.1
  143.0 11.1 %conditional.4 = ((f32[4,4,256]{2,1,0:T(4,128)S(1)}, f32[4,4,256]{2,1,0:T(4,128)S(1)}, f32[4,4,256,128]{3,2,1,0:T(8,128)})) conditional(s32[]{:T(128)} %convert_element_type.38, (f32[4,4,256]{2,1,0:T(4,128)S(1)}, f32[4,4,256]{2,1,0:T(4,128)S(1)}, f32[4,4,256,128]{3,2,1,0:T(8,128)}) %tuple.84, (pred[256,512]{0,1:T(8,128)(4,1)S(1)}, ...), branch_computations={%region_3.3_spmd, %region_4.6_spmd} | conditional | flops 1098915840 | bytes 54526076 | solution.py:71
  145.7 1.9 fusion.6
  147.6 1.8 fusion.10
  149.5 3.3 %multiply_add_fusion = f32[4,4,256,128]{3,2,1,0:T(8,128)S(1)} fusion(f32[4,4,256,128]{3,2,1,0:T(8,128)S(1)} %copy-done, bf16[512,4,128,1]{0,2,3,1:T(8,128)(2,1)S(1)} %bitcast.53, f32[4,512,256,4]{2,1,3,0:T(8,128)S(1)} %get-tuple-element.534, f32[4,4,256]{2,1,0:T(4,128)S(1)} %max.5, pred[4,256,512]{1,2,0:T(8,128)(4,1)S(1)} %and_or_fusion, ...), kind=kOutput, calls=%fused_computation.15 | convolution fusion | flops 546308096 | bytes 13664256 | tf_op jit(solution)/shard_map/while/body/eval_jaxpr/cond/branch_1_fun/gjqk,kgd->gjqd/dot_general | solution.py:58
  152.8 1.3 copy-done.1
  157.9 11.1 %conditional.4 = ((f32[4,4,256]{2,1,0:T(4,128)S(1)}, f32[4,4,256]{2,1,0:T(4,128)S(1)}, f32[4,4,256,128]{3,2,1,0:T(8,128)})) conditional(s32[]{:T(128)} %convert_element_type.38, (f32[4,4,256]{2,1,0:T(4,128)S(1)}, f32[4,4,256]{2,1,0:T(4,128)S(1)}, f32[4,4,256,128]{3,2,1,0:T(8,128)}) %tuple.84, (pred[256,512]{0,1:T(8,128)(4,1)S(1)}, ...), branch_computations={%region_3.3_spmd, %region_4.6_spmd} | conditional | flops 1098915840 | bytes 54526076 | solution.py:71
  160.5 1.9 fusion.6
  162.5 1.8 fusion.10
  164.3 3.3 %multiply_add_fusion = f32[4,4,256,128]{3,2,1,0:T(8,128)S(1)} fusion(f32[4,4,256,128]{3,2,1,0:T(8,128)S(1)} %copy-done, bf16[512,4,128,1]{0,2,3,1:T(8,128)(2,1)S(1)} %bitcast.53, f32[4,512,256,4]{2,1,3,0:T(8,128)S(1)} %get-tuple-element.534, f32[4,4,256]{2,1,0:T(4,128)S(1)} %max.5, pred[4,256,512]{1,2,0:T(8,128)(4,1)S(1)} %and_or_fusion, ...), kind=kOutput, calls=%fused_computation.15 | convolution fusion | flops 546308096 | bytes 13664256 | tf_op jit(solution)/shard_map/while/body/eval_jaxpr/cond/branch_1_fun/gjqk,kgd->gjqd/dot_general | solution.py:58
  167.7 1.3 copy-done.1
  172.7 11.1 %conditional.4 = ((f32[4,4,256]{2,1,0:T(4,128)S(1)}, f32[4,4,256]{2,1,0:T(4,128)S(1)}, f32[4,4,256,128]{3,2,1,0:T(8,128)})) conditional(s32[]{:T(128)} %convert_element_type.38, (f32[4,4,256]{2,1,0:T(4,128)S(1)}, f32[4,4,256]{2,1,0:T(4,128)S(1)}, f32[4,4,256,128]{3,2,1,0:T(8,128)}) %tuple.84, (pred[256,512]{0,1:T(8,128)(4,1)S(1)}, ...), branch_computations={%region_3.3_spmd, %region_4.6_spmd} | conditional | flops 1098915840 | bytes 54526076 | solution.py:71
  175.4 1.9 fusion.6
  177.3 1.8 fusion.10
  179.2 3.3 %multiply_add_fusion = f32[4,4,256,128]{3,2,1,0:T(8,128)S(1)} fusion(f32[4,4,256,128]{3,2,1,0:T(8,128)S(1)} %copy-done, bf16[512,4,128,1]{0,2,3,1:T(8,128)(2,1)S(1)} %bitcast.53, f32[4,512,256,4]{2,1,3,0:T(8,128)S(1)} %get-tuple-element.534, f32[4,4,256]{2,1,0:T(4,128)S(1)} %max.5, pred[4,256,512]{1,2,0:T(8,128)(4,1)S(1)} %and_or_fusion, ...), kind=kOutput, calls=%fused_computation.15 | convolution fusion | flops 546308096 | bytes 13664256 | tf_op jit(solution)/shard_map/while/body/eval_jaxpr/cond/branch_1_fun/gjqk,kgd->gjqd/dot_general | solution.py:58
  182.5 1.3 copy-done.1
  187.6 11.1 %conditional.4 = ((f32[4,4,256]{2,1,0:T(4,128)S(1)}, f32[4,4,256]{2,1,0:T(4,128)S(1)}, f32[4,4,256,128]{3,2,1,0:T(8,128)})) conditional(s32[]{:T(128)} %convert_element_type.38, (f32[4,4,256]{2,1,0:T(4,128)S(1)}, f32[4,4,256]{2,1,0:T(4,128)S(1)}, f32[4,4,256,128]{3,2,1,0:T(8,128)}) %tuple.84, (pred[256,512]{0,1:T(8,128)(4,1)S(1)}, ...), branch_computations={%region_3.3_spmd, %region_4.6_spmd} | conditional | flops 1098915840 | bytes 54526076 | solution.py:71
  190.2 1.9 fusion.6
  192.2 1.8 fusion.10
  194.0 3.3 %multiply_add_fusion = f32[4,4,256,128]{3,2,1,0:T(8,128)S(1)} fusion(f32[4,4,256,128]{3,2,1,0:T(8,128)S(1)} %copy-done, bf16[512,4,128,1]{0,2,3,1:T(8,128)(2,1)S(1)} %bitcast.53, f32[4,512,256,4]{2,1,3,0:T(8,128)S(1)} %get-tuple-element.534, f32[4,4,256]{2,1,0:T(4,128)S(1)} %max.5, pred[4,256,512]{1,2,0:T(8,128)(4,1)S(1)} %and_or_fusion, ...), kind=kOutput, calls=%fused_computation.15 | convolution fusion | flops 546308096 | bytes 13664256 | tf_op jit(solution)/shard_map/while/body/eval_jaxpr/cond/branch_1_fun/gjqk,kgd->gjqd/dot_general | solution.py:58
  202.4 11.1 %conditional.4 = ((f32[4,4,256]{2,1,0:T(4,128)S(1)}, f32[4,4,256]{2,1,0:T(4,128)S(1)}, f32[4,4,256,128]{3,2,1,0:T(8,128)})) conditional(s32[]{:T(128)} %convert_element_type.38, (f32[4,4,256]{2,1,0:T(4,128)S(1)}, f32[4,4,256]{2,1,0:T(4,128)S(1)}, f32[4,4,256,128]{3,2,1,0:T(8,128)}) %tuple.84, (pred[256,512]{0,1:T(8,128)(4,1)S(1)}, ...), branch_computations={%region_3.3_spmd, %region_4.6_spmd} | conditional | flops 1098915840 | bytes 54526076 | solution.py:71
  205.1 1.9 fusion.6
  207.0 1.8 fusion.10
  208.9 3.3 %multiply_add_fusion = f32[4,4,256,128]{3,2,1,0:T(8,128)S(1)} fusion(f32[4,4,256,128]{3,2,1,0:T(8,128)S(1)} %copy-done, bf16[512,4,128,1]{0,2,3,1:T(8,128)(2,1)S(1)} %bitcast.53, f32[4,512,256,4]{2,1,3,0:T(8,128)S(1)} %get-tuple-element.534, f32[4,4,256]{2,1,0:T(4,128)S(1)} %max.5, pred[4,256,512]{1,2,0:T(8,128)(4,1)S(1)} %and_or_fusion, ...), kind=kOutput, calls=%fused_computation.15 | convolution fusion | flops 546308096 | bytes 13664256 | tf_op jit(solution)/shard_map/while/body/eval_jaxpr/cond/branch_1_fun/gjqk,kgd->gjqd/dot_general | solution.py:58
  217.3 11.1 %conditional.4 = ((f32[4,4,256]{2,1,0:T(4,128)S(1)}, f32[4,4,256]{2,1,0:T(4,128)S(1)}, f32[4,4,256,128]{3,2,1,0:T(8,128)})) conditional(s32[]{:T(128)} %convert_element_type.38, (f32[4,4,256]{2,1,0:T(4,128)S(1)}, f32[4,4,256]{2,1,0:T(4,128)S(1)}, f32[4,4,256,128]{3,2,1,0:T(8,128)}) %tuple.84, (pred[256,512]{0,1:T(8,128)(4,1)S(1)}, ...), branch_computations={%region_3.3_spmd, %region_4.6_spmd} | conditional | flops 1098915840 | bytes 54526076 | solution.py:71
  219.9 1.9 fusion.6
  221.9 1.8 fusion.10
  223.7 3.3 %multiply_add_fusion = f32[4,4,256,128]{3,2,1,0:T(8,128)S(1)} fusion(f32[4,4,256,128]{3,2,1,0:T(8,128)S(1)} %copy-done, bf16[512,4,128,1]{0,2,3,1:T(8,128)(2,1)S(1)} %bitcast.53, f32[4,512,256,4]{2,1,3,0:T(8,128)S(1)} %get-tuple-element.534, f32[4,4,256]{2,1,0:T(4,128)S(1)} %max.5, pred[4,256,512]{1,2,0:T(8,128)(4,1)S(1)} %and_or_fusion, ...), kind=kOutput, calls=%fused_computation.15 | convolution fusion | flops 546308096 | bytes 13664256 | tf_op jit(solution)/shard_map/while/body/eval_jaxpr/cond/branch_1_fun/gjqk,kgd->gjqd/dot_general | solution.py:58
  227.1 1.3 copy-done.1
  232.1 11.1 %conditional.4 = ((f32[4,4,256]{2,1,0:T(4,128)S(1)}, f32[4,4,256]{2,1,0:T(4,128)S(1)}, f32[4,4,256,128]{3,2,1,0:T(8,128)})) conditional(s32[]{:T(128)} %convert_element_type.38, (f32[4,4,256]{2,1,0:T(4,128)S(1)}, f32[4,4,256]{2,1,0:T(4,128)S(1)}, f32[4,4,256,128]{3,2,1,0:T(8,128)}) %tuple.84, (pred[256,512]{0,1:T(8,128)(4,1)S(1)}, ...), branch_computations={%region_3.3_spmd, %region_4.6_spmd} | conditional | flops 1098915840 | bytes 54526076 | solution.py:71
  234.8 1.9 fusion.6
  236.7 1.8 fusion.10
  238.6 3.3 %multiply_add_fusion = f32[4,4,256,128]{3,2,1,0:T(8,128)S(1)} fusion(f32[4,4,256,128]{3,2,1,0:T(8,128)S(1)} %copy-done, bf16[512,4,128,1]{0,2,3,1:T(8,128)(2,1)S(1)} %bitcast.53, f32[4,512,256,4]{2,1,3,0:T(8,128)S(1)} %get-tuple-element.534, f32[4,4,256]{2,1,0:T(4,128)S(1)} %max.5, pred[4,256,512]{1,2,0:T(8,128)(4,1)S(1)} %and_or_fusion, ...), kind=kOutput, calls=%fused_computation.15 | convolution fusion | flops 546308096 | bytes 13664256 | tf_op jit(solution)/shard_map/while/body/eval_jaxpr/cond/branch_1_fun/gjqk,kgd->gjqd/dot_general | solution.py:58
  241.9 1.3 copy-done.1
  243.3 1.9 fusion.24
  246.0 1.6 convert_element_type.27
  (170 shorter events, 55.1 us)
Async XLA Ops:
  6.5 18.1 %copy-start.2 = (bf16[256,2048]{1,0:T(8,128)(2,1)S(1)}, bf16[256,2048]{1,0:T(8,128)(2,1)}, u32[]{:S(2)}) copy-start(bf16[256,2048]{1,0:T(8,128)(2,1)} %param.8) | copy-start | bytes 3145732
  6.5 58.6 %all-gather.3.cloned.1.call-start = ((), (), s32[]{:S(2)}) async-start(), calls=%async_computation.2 | async-start | bytes 4456448 | tf_op jit(solution)/shard_map/all_gather | solution.py:76
  15.4 101.1 %all-gather.5.cloned.1.call-start = ((), (), s32[]{:S(2)}) async-start(), calls=%async_computation.3 | async-start | bytes 4456448 | tf_op jit(solution)/shard_map/all_gather | solution.py:77
  132.8 1.9 copy-start
  138.0 1.4 copy-start.1
  147.6 1.9 copy-start
  152.8 1.4 copy-start.1
  162.5 1.9 copy-start
  167.7 1.4 copy-start.1
  177.3 1.9 copy-start
  182.5 1.4 copy-start.1
  192.1 1.9 copy-start
  197.4 1.4 copy-start.1
  207.0 1.9 copy-start
  212.2 1.4 copy-start.1
  221.8 1.9 copy-start
  227.1 1.4 copy-start.1
  236.7 1.9 copy-start
  241.9 1.4 copy-start.1
Sparse Core Ops, SparseCore 0:
  15.5 49.6 all-gather.2
  67.3 49.0 all-gather.4
where the time goes:
time: 255 us; the launch traced here: 254 us
  waiting for transfers between devices  84.2 us (33%)
  local copies, waits for them, and re-layouts  56.3 us (22%)
  matrix products  41.6 us (16%)
  other arithmetic  39.5 us (15%)
  between operations  13.5 us (5%)
  blocking collectives  13.1 us (5%)
  loops' own time  6.12 us (2%)
    all_gather x1, waiting for transfers between devices, body(): value_piece = lax.all_gather(own_values, 'ctx', axis=0, tiled=True)  44.8 us
    all_gather x1, waiting for transfers between devices, body(): key_piece = lax.all_gather(own_keys, 'ctx', axis=0, tiled=True)  39.4 us
    dot_general x8, matrix products, compute(): jnp.einsum('gjqk,kgd->gjqd', weights.astype(jnp.bfloat16), value_rows.res...  26.6 us
    unnamed x9, local copies, waits for them, and re-layouts  17.2 us
    dot_general x8, matrix products, compute(): jnp.einsum('qgjd,kgd->gjqk', query_four, key_rows.reshape(row_count, grou...  15.1 us
    reduce_sum x8, other arithmetic, compute(): totals = totals * factor + jnp.sum(weights, axis=-1)  14.7 us
    cond x40, local copies, waits for them, and re-layouts  10.8 us
    dynamic_slice x8, local copies, waits for them, and re-layouts, loop_body(): lax.dynamic_slice_in_dim(value_piece, block_index * step_rows, step_rows, 0)  10.2 us
  transfers between devices with their start and end apart: 2, of which 2 were waited for; matrix products, arithmetic and copies ran while one was open for 4% of the time, Pallas kernels for 0%

commit v1 on v0

--- a/solution.py
+++ b/solution.py
@@ -10,6 +10,12 @@
 BLK = 512
 TILE = 128
 floor_value = -1e30
+
+
+def in_order(blocks, dim):
+    shape = list(blocks.shape[1:])
+    shape[dim] *= blocks.shape[0]
+    return jnp.moveaxis(blocks, 0, dim).reshape(shape)
 
 
 def body(queries, keys, values, selected):
@@ -74,7 +80,19 @@
     start_totals = jnp.zeros((group_count, per_group, local_rows), jnp.float32)
     start_accumulated = jnp.zeros((group_count, per_group, local_rows, HD), jnp.float32)
     key_piece = lax.all_gather(own_keys, "ctx", axis=0, tiled=True)
-    value_piece = lax.all_gather(own_values, "ctx", axis=0, tiled=True)
+    size = lax.axis_size("ctx")
+    pairs = [(i, (i + 1) % size) for i in range(size)]
+    back = [(b, a) for a, b in pairs]
+    lower, upper = ([], [])
+    for step in range(size - 1):
+        if step % 2 == 0:
+            lower.append(lax.ppermute(lower[-1] if lower else own_values, "ctx", pairs))
+        else:
+            upper.append(lax.ppermute(upper[-1] if upper else own_values, "ctx", back))
+    parts = jnp.stack([*lower[::-1], own_values, *upper])
+    shift = lax.axis_index("ctx") - len(lower)
+    parts = parts[(jnp.arange(size) - shift) % size]
+    value_piece = in_order(parts, 0)
     row_count = key_piece.shape[0]
     step_rows = math.gcd(row_count, 512)
 

time: 255 us -> 272 us (1.067)
  waiting for transfers between devices: 84.2 us -> 36.6 us
  starting transfers between devices: 0.04 us -> 39.6 us
  local copies, waits for them, and re-layouts: 56.3 us -> 80.5 us
    all_gather x1 -> x0, waiting for transfers between devices: 44.8 us -> none  [body(): value_piece = lax.all_gather(own_values, 'ctx', axis=0, tiled=True)]
    ppermute x0 -> x15, starting transfers between devices: none -> 39.6 us  [the longest x8 39.5 us: body(): lower.append(lax.ppermute(lower[-1] if lower else own_values, 'ctx', pairs))]
    all_gather x1, waiting for transfers between devices: 39.4 us -> 0.01 us  [body(): key_piece = lax.all_gather(own_keys, 'ctx', axis=0, tiled=True)]
    ppermute x0 -> x15, waiting for transfers between devices: none -> 36.5 us  [the longest x8 29.8 us: body(): lower.append(lax.ppermute(lower[-1] if lower else own_values, 'ctx', pairs))]
    unnamed x9 -> x38, local copies, waits for them, and re-layouts: 17.2 us -> 36.6 us
    gather x0 -> x1, local copies, waits for them, and re-layouts: none -> 4.98 us  [body(): parts = parts[(jnp.arange(size) - shift) % size]]
    another operation x8 -> x9, local copies, waits for them, and re-layouts: 7.71 us -> 8.48 us
  transfers between devices with their start and end apart: 2 -> 16, of which waited for: 2 -> 12; matrix products, arithmetic and copies ran while one was open for 4% -> 13% of each run, Pallas kernels for 0% -> 0%
where the time goes in v1:
time: 272 us; the launch traced here: 271 us
  local copies, waits for them, and re-layouts  80.5 us (30%)
  matrix products  41.6 us (15%)
  other arithmetic  39.7 us (15%)
  starting transfers between devices  39.6 us (15%)
  waiting for transfers between devices  36.6 us (13%)
  between operations  13.6 us (5%)
  blocking collectives  13.1 us (5%)
  loops' own time  6.07 us (2%)
    ppermute x8, starting transfers between devices, body(): lower.append(lax.ppermute(lower[-1] if lower else own_values, 'ctx', pairs))  39.5 us
    unnamed x38, local copies, waits for them, and re-layouts  36.6 us
    ppermute x8, waiting for transfers between devices, body(): lower.append(lax.ppermute(lower[-1] if lower else own_values, 'ctx', pairs))  29.8 us
    dot_general x8, matrix products, compute(): jnp.einsum('gjqk,kgd->gjqd', weights.astype(jnp.bfloat16), value_rows.res...  26.6 us
    dot_general x8, matrix products, compute(): jnp.einsum('qgjd,kgd->gjqk', query_four, key_rows.reshape(row_count, grou...  15 us
    reduce_sum x8, other arithmetic, compute(): totals = totals * factor + jnp.sum(weights, axis=-1)  14.7 us
    cond x40, local copies, waits for them, and re-layouts  10.6 us
    dynamic_slice x8, local copies, waits for them, and re-layouts, loop_body(): lax.dynamic_slice_in_dim(value_piece, block_index * step_rows, step_rows, 0)  10.2 us
  transfers between devices with their start and end apart: 16, of which 12 were waited for; matrix products, arithmetic and copies ran while one was open for 13% of the time, Pallas kernels for 0%

profile of v1, /device:TPU:27, one launch (start us, length us, event | category | flops | bytes accessed | tf_op | source)
XLA Modules:
  0.0 270.8 jit_solution(15227981520309815129)
XLA Ops:
  7.7 6.7 %all_to_all.38 = bf16[128,2,512]{0,2,1:T(8,128)(2,1)S(1)} all-to-all(bf16[128,2,512]{0,2,1:T(8,128)(2,1)S(1)} %bitcast.99), channel_id=1, replica_groups=mesh['ctx'=16,'head'=2] {'head'}, dimensions={1} | all-to-all | bytes 524288 | tf_op jit(solution)/shard_map/all_to_all | solution.py:27
  16.4 6.4 %all_to_all.39 = bf16[128,2,512]{0,2,1:T(8,128)(2,1)S(1)} all-to-all(bf16[128,2,512]{0,2,1:T(8,128)(2,1)S(1)} %bitcast.100), channel_id=1, replica_groups=mesh['ctx'=16,'head'=2] {'head'}, dimensions={1} | all-to-all | bytes 524288 | tf_op jit(solution)/shard_map/all_to_all | solution.py:28
  23.0 2.7 collective-permute-start
  25.7 8.7 %collective-permute-done = bf16[256,512]{1,0:T(8,128)(2,1)S(1)} collective-permute-done((bf16[256,512]{1,0:T(8,128)(2,1)S(1)}, bf16[256,512]{1,0:T(8,128)(2,1)S(1)}, u32[]{:S(2)}, u32[]{:S(2)}) %collective-permute-start) | collective-permute-done | bytes 262176 | tf_op jit(solution)/shard_map/ppermute | solution.py:89
  34.3 5.2 %collective-permute-start.1 = (bf16[256,512]{1,0:T(8,128)(2,1)S(1)}, bf16[256,512]{1,0:T(8,128)(2,1)S(1)}, u32[]{:S(2)}, u32[]{:S(2)}) collective-permute-start(bf16[256,512]{1,0:T(8,128)(2,1)S(1)} %collective-permute-done), channel_id=1, source_target_pairs={{0,2},{2,4},{4,6},{6,8},{8,10},{10,12},{12,14},{14,16},{16,18},{18... | collective-permute-start | bytes 786440 | tf_op jit(solution)/shard_map/ppermute | solution.py:89
  39.5 3.3 %collective-permute-done.1 = bf16[256,512]{1,0:T(8,128)(2,1)S(1)} collective-permute-done((bf16[256,512]{1,0:T(8,128)(2,1)S(1)}, bf16[256,512]{1,0:T(8,128)(2,1)S(1)}, u32[]{:S(2)}, u32[]{:S(2)}) %collective-permute-start.1) | collective-permute-done | bytes 262176 | tf_op jit(solution)/shard_map/ppermute | solution.py:89
  42.8 5.3 %collective-permute-start.2 = (bf16[256,512]{1,0:T(8,128)(2,1)S(1)}, bf16[256,512]{1,0:T(8,128)(2,1)S(1)}, u32[]{:S(2)}, u32[]{:S(2)}) collective-permute-start(bf16[256,512]{1,0:T(8,128)(2,1)S(1)} %collective-permute-done.1), channel_id=1, source_target_pairs={{0,2},{2,4},{4,6},{6,8},{8,10},{10,12},{12,14},{14,16},{16,18},{18... | collective-permute-start | bytes 786440 | tf_op jit(solution)/shard_map/ppermute | solution.py:89
  49.4 7.5 %collective-permute-done.2 = bf16[256,512]{1,0:T(8,128)(2,1)S(1)} collective-permute-done((bf16[256,512]{1,0:T(8,128)(2,1)S(1)}, bf16[256,512]{1,0:T(8,128)(2,1)S(1)}, u32[]{:S(2)}, u32[]{:S(2)}) %collective-permute-start.2) | collective-permute-done | bytes 262176 | tf_op jit(solution)/shard_map/ppermute | solution.py:89
  56.9 5.2 %collective-permute-start.3 = (bf16[256,512]{1,0:T(8,128)(2,1)S(1)}, bf16[256,512]{1,0:T(8,128)(2,1)S(1)}, u32[]{:S(2)}, u32[]{:S(2)}) collective-permute-start(bf16[256,512]{1,0:T(8,128)(2,1)S(1)} %collective-permute-done.2), channel_id=1, source_target_pairs={{0,2},{2,4},{4,6},{6,8},{8,10},{10,12},{12,14},{14,16},{16,18},{18... | collective-permute-start | bytes 786440 | tf_op jit(solution)/shard_map/ppermute | solution.py:89
  62.1 4.7 %collective-permute-done.3 = bf16[256,512]{1,0:T(8,128)(2,1)S(1)} collective-permute-done((bf16[256,512]{1,0:T(8,128)(2,1)S(1)}, bf16[256,512]{1,0:T(8,128)(2,1)S(1)}, u32[]{:S(2)}, u32[]{:S(2)}) %collective-permute-start.3) | collective-permute-done | bytes 262176 | tf_op jit(solution)/shard_map/ppermute | solution.py:89
  66.9 5.3 %collective-permute-start.4 = (bf16[256,512]{1,0:T(8,128)(2,1)S(1)}, bf16[256,512]{1,0:T(8,128)(2,1)S(1)}, u32[]{:S(2)}, u32[]{:S(2)}) collective-permute-start(bf16[256,512]{1,0:T(8,128)(2,1)S(1)} %collective-permute-done.3), channel_id=1, source_target_pairs={{0,2},{2,4},{4,6},{6,8},{8,10},{10,12},{12,14},{14,16},{16,18},{18... | collective-permute-start | bytes 786440 | tf_op jit(solution)/shard_map/ppermute | solution.py:89
  72.1 2.2 collective-permute-done.10
  76.0 5.3 %collective-permute-start.5 = (bf16[256,512]{1,0:T(8,128)(2,1)S(1)}, bf16[256,512]{1,0:T(8,128)(2,1)S(1)}, u32[]{:S(2)}, u32[]{:S(2)}) collective-permute-start(bf16[256,512]{1,0:T(8,128)(2,1)S(1)} %collective-permute-done.4), channel_id=1, source_target_pairs={{0,2},{2,4},{4,6},{6,8},{8,10},{10,12},{12,14},{14,16},{16,18},{18... | collective-permute-start | bytes 786440 | tf_op jit(solution)/shard_map/ppermute | solution.py:89
  84.6 5.3 %collective-permute-start.6 = (bf16[256,512]{1,0:T(8,128)(2,1)S(1)}, bf16[256,512]{1,0:T(8,128)(2,1)}, u32[]{:S(2)}, u32[]{:S(2)}) collective-permute-start(bf16[256,512]{1,0:T(8,128)(2,1)S(1)} %collective-permute-done.5), channel_id=1, source_target_pairs={{0,2},{2,4},{4,6},{6,8},{8,10},{10,12},{12,14},{14,16},{16,18},{18... | collective-permute-start | bytes 786440 | tf_op jit(solution)/shard_map/ppermute | solution.py:89
  93.2 5.3 %collective-permute-start.7 = (bf16[256,512]{1,0:T(8,128)(2,1)}, bf16[256,512]{1,0:T(8,128)(2,1)}, u32[]{:S(2)}, u32[]{:S(2)}) collective-permute-start(bf16[256,512]{1,0:T(8,128)(2,1)} %collective-permute-done.6), channel_id=1, source_target_pairs={{0,2},{2,4},{4,6},{6,8},{8,10},{10,12},{12,14},{14,16},{16,18},{18... | collective-permute-start | bytes 786440 | tf_op jit(solution)/shard_map/ppermute | solution.py:89
  121.4 5.0 %gather_fusion = bf16[16,256,512]{2,1,0:T(8,128)(2,1)} fusion(bf16[16,256,512]{2,1,0:T(8,128)(2,1)} %bitcast_dynamic-update-slice_fusion, s32[1024]{0:T(1024)S(1)} %pad_clamp_fusion), kind=kCustom, calls=%fused_computation | custom fusion | bytes 8388672 | tf_op jit(solution)/shard_map/gather | solution.py:94
  126.4 6.5 %copy.88 = bf16[4096,512]{0,1:T(8,128)(2,1)} copy(bf16[4096,512]{1,0:T(8,128)(2,1)} %bitcast.88) | data formatting | bytes 8388608
  132.9 6.4 %copy.86 = bf16[4096,512]{0,1:T(8,128)(2,1)} copy(bf16[4096,512]{1,0:T(8,128)(2,1)} %all-gather.2.cloned.1.call-done) | data formatting | bytes 8388608
  140.9 118.7 %while.21 = (s32[]{:T(128)}, f32[4,4,256]{2,1,0:T(4,128)S(1)}, f32[4,4,256]{2,1,0:T(4,128)S(1)}, f32[4,4,256,128]{3,2,1,0:T(8,128)}, bf16[4096,512]{0,1:T(8,128)...) while((s32[]{:T(128)}, f32[4,4,256]{2,1,0:T(4,128)S(1)}, ...), condition=%wide.region_7.8_spmd.clone.clone, body=%wide.region_0.7_spmd.clone.clone.sunk | while | flops 1103646720 | bytes 56711624 | solution.py:104
  144.6 11.1 %conditional.4 = ((f32[4,4,256]{2,1,0:T(4,128)S(1)}, f32[4,4,256]{2,1,0:T(4,128)S(1)}, f32[4,4,256,128]{3,2,1,0:T(8,128)})) conditional(s32[]{:T(128)} %convert_element_type.38, (f32[4,4,256]{2,1,0:T(4,128)S(1)}, f32[4,4,256]{2,1,0:T(4,128)S(1)}, f32[4,4,256,128]{3,2,1,0:T(8,128)}) %tuple.85, (pred[256,512]{0,1:T(8,128)(4,1)S(1)}, ...), branch_computations={%region_3.3_spmd, %region_4.6_spmd} | conditional | flops 1098915840 | bytes 54526076 | solution.py:77
  147.3 1.9 fusion.6
  149.2 1.8 fusion.10
  151.1 3.3 %multiply_add_fusion = f32[4,4,256,128]{3,2,1,0:T(8,128)S(1)} fusion(f32[4,4,256,128]{3,2,1,0:T(8,128)S(1)} %copy-done, bf16[512,4,128,1]{0,2,3,1:T(8,128)(2,1)S(1)} %bitcast.89, f32[4,512,256,4]{2,1,3,0:T(8,128)S(1)} %get-tuple-element.543, f32[4,4,256]{2,1,0:T(4,128)S(1)} %max.5, pred[4,256,512]{1,2,0:T(8,128)(4,1)S(1)} %and_or_fusion, ...), kind=kOutput, calls=%fused_computation.16 | convolution fusion | flops 546308096 | bytes 13664256 | tf_op jit(solution)/shard_map/while/body/eval_jaxpr/cond/branch_1_fun/gjqk,kgd->gjqd/dot_general | solution.py:64
  159.4 11.1 %conditional.4 = ((f32[4,4,256]{2,1,0:T(4,128)S(1)}, f32[4,4,256]{2,1,0:T(4,128)S(1)}, f32[4,4,256,128]{3,2,1,0:T(8,128)})) conditional(s32[]{:T(128)} %convert_element_type.38, (f32[4,4,256]{2,1,0:T(4,128)S(1)}, f32[4,4,256]{2,1,0:T(4,128)S(1)}, f32[4,4,256,128]{3,2,1,0:T(8,128)}) %tuple.85, (pred[256,512]{0,1:T(8,128)(4,1)S(1)}, ...), branch_computations={%region_3.3_spmd, %region_4.6_spmd} | conditional | flops 1098915840 | bytes 54526076 | solution.py:77
  162.1 1.9 fusion.6
  164.0 1.8 fusion.10
  165.9 3.3 %multiply_add_fusion = f32[4,4,256,128]{3,2,1,0:T(8,128)S(1)} fusion(f32[4,4,256,128]{3,2,1,0:T(8,128)S(1)} %copy-done, bf16[512,4,128,1]{0,2,3,1:T(8,128)(2,1)S(1)} %bitcast.89, f32[4,512,256,4]{2,1,3,0:T(8,128)S(1)} %get-tuple-element.543, f32[4,4,256]{2,1,0:T(4,128)S(1)} %max.5, pred[4,256,512]{1,2,0:T(8,128)(4,1)S(1)} %and_or_fusion, ...), kind=kOutput, calls=%fused_computation.16 | convolution fusion | flops 546308096 | bytes 13664256 | tf_op jit(solution)/shard_map/while/body/eval_jaxpr/cond/branch_1_fun/gjqk,kgd->gjqd/dot_general | solution.py:64
  174.3 11.1 %conditional.4 = ((f32[4,4,256]{2,1,0:T(4,128)S(1)}, f32[4,4,256]{2,1,0:T(4,128)S(1)}, f32[4,4,256,128]{3,2,1,0:T(8,128)})) conditional(s32[]{:T(128)} %convert_element_type.38, (f32[4,4,256]{2,1,0:T(4,128)S(1)}, f32[4,4,256]{2,1,0:T(4,128)S(1)}, f32[4,4,256,128]{3,2,1,0:T(8,128)}) %tuple.85, (pred[256,512]{0,1:T(8,128)(4,1)S(1)}, ...), branch_computations={%region_3.3_spmd, %region_4.6_spmd} | conditional | flops 1098915840 | bytes 54526076 | solution.py:77
  176.9 1.9 fusion.6
  178.9 1.8 fusion.10
  180.7 3.3 %multiply_add_fusion = f32[4,4,256,128]{3,2,1,0:T(8,128)S(1)} fusion(f32[4,4,256,128]{3,2,1,0:T(8,128)S(1)} %copy-done, bf16[512,4,128,1]{0,2,3,1:T(8,128)(2,1)S(1)} %bitcast.89, f32[4,512,256,4]{2,1,3,0:T(8,128)S(1)} %get-tuple-element.543, f32[4,4,256]{2,1,0:T(4,128)S(1)} %max.5, pred[4,256,512]{1,2,0:T(8,128)(4,1)S(1)} %and_or_fusion, ...), kind=kOutput, calls=%fused_computation.16 | convolution fusion | flops 546308096 | bytes 13664256 | tf_op jit(solution)/shard_map/while/body/eval_jaxpr/cond/branch_1_fun/gjqk,kgd->gjqd/dot_general | solution.py:64
  189.1 11.1 %conditional.4 = ((f32[4,4,256]{2,1,0:T(4,128)S(1)}, f32[4,4,256]{2,1,0:T(4,128)S(1)}, f32[4,4,256,128]{3,2,1,0:T(8,128)})) conditional(s32[]{:T(128)} %convert_element_type.38, (f32[4,4,256]{2,1,0:T(4,128)S(1)}, f32[4,4,256]{2,1,0:T(4,128)S(1)}, f32[4,4,256,128]{3,2,1,0:T(8,128)}) %tuple.85, (pred[256,512]{0,1:T(8,128)(4,1)S(1)}, ...), branch_computations={%region_3.3_spmd, %region_4.6_spmd} | conditional | flops 1098915840 | bytes 54526076 | solution.py:77
  191.8 1.9 fusion.6
  193.7 1.8 fusion.10
  195.6 3.3 %multiply_add_fusion = f32[4,4,256,128]{3,2,1,0:T(8,128)S(1)} fusion(f32[4,4,256,128]{3,2,1,0:T(8,128)S(1)} %copy-done, bf16[512,4,128,1]{0,2,3,1:T(8,128)(2,1)S(1)} %bitcast.89, f32[4,512,256,4]{2,1,3,0:T(8,128)S(1)} %get-tuple-element.543, f32[4,4,256]{2,1,0:T(4,128)S(1)} %max.5, pred[4,256,512]{1,2,0:T(8,128)(4,1)S(1)} %and_or_fusion, ...), kind=kOutput, calls=%fused_computation.16 | convolution fusion | flops 546308096 | bytes 13664256 | tf_op jit(solution)/shard_map/while/body/eval_jaxpr/cond/branch_1_fun/gjqk,kgd->gjqd/dot_general | solution.py:64
  204.0 11.1 %conditional.4 = ((f32[4,4,256]{2,1,0:T(4,128)S(1)}, f32[4,4,256]{2,1,0:T(4,128)S(1)}, f32[4,4,256,128]{3,2,1,0:T(8,128)})) conditional(s32[]{:T(128)} %convert_element_type.38, (f32[4,4,256]{2,1,0:T(4,128)S(1)}, f32[4,4,256]{2,1,0:T(4,128)S(1)}, f32[4,4,256,128]{3,2,1,0:T(8,128)}) %tuple.85, (pred[256,512]{0,1:T(8,128)(4,1)S(1)}, ...), branch_computations={%region_3.3_spmd, %region_4.6_spmd} | conditional | flops 1098915840 | bytes 54526076 | solution.py:77
  206.6 1.9 fusion.6
  210.4 3.3 %multiply_add_fusion = f32[4,4,256,128]{3,2,1,0:T(8,128)S(1)} fusion(f32[4,4,256,128]{3,2,1,0:T(8,128)S(1)} %copy-done, bf16[512,4,128,1]{0,2,3,1:T(8,128)(2,1)S(1)} %bitcast.89, f32[4,512,256,4]{2,1,3,0:T(8,128)S(1)} %get-tuple-element.543, f32[4,4,256]{2,1,0:T(4,128)S(1)} %max.5, pred[4,256,512]{1,2,0:T(8,128)(4,1)S(1)} %and_or_fusion, ...), kind=kOutput, calls=%fused_computation.16 | convolution fusion | flops 546308096 | bytes 13664256 | tf_op jit(solution)/shard_map/while/body/eval_jaxpr/cond/branch_1_fun/gjqk,kgd->gjqd/dot_general | solution.py:64
  218.8 11.1 %conditional.4 = ((f32[4,4,256]{2,1,0:T(4,128)S(1)}, f32[4,4,256]{2,1,0:T(4,128)S(1)}, f32[4,4,256,128]{3,2,1,0:T(8,128)})) conditional(s32[]{:T(128)} %convert_element_type.38, (f32[4,4,256]{2,1,0:T(4,128)S(1)}, f32[4,4,256]{2,1,0:T(4,128)S(1)}, f32[4,4,256,128]{3,2,1,0:T(8,128)}) %tuple.85, (pred[256,512]{0,1:T(8,128)(4,1)S(1)}, ...), branch_computations={%region_3.3_spmd, %region_4.6_spmd} | conditional | flops 1098915840 | bytes 54526076 | solution.py:77
  221.5 1.9 fusion.6
  225.2 3.3 %multiply_add_fusion = f32[4,4,256,128]{3,2,1,0:T(8,128)S(1)} fusion(f32[4,4,256,128]{3,2,1,0:T(8,128)S(1)} %copy-done, bf16[512,4,128,1]{0,2,3,1:T(8,128)(2,1)S(1)} %bitcast.89, f32[4,512,256,4]{2,1,3,0:T(8,128)S(1)} %get-tuple-element.543, f32[4,4,256]{2,1,0:T(4,128)S(1)} %max.5, pred[4,256,512]{1,2,0:T(8,128)(4,1)S(1)} %and_or_fusion, ...), kind=kOutput, calls=%fused_computation.16 | convolution fusion | flops 546308096 | bytes 13664256 | tf_op jit(solution)/shard_map/while/body/eval_jaxpr/cond/branch_1_fun/gjqk,kgd->gjqd/dot_general | solution.py:64
  233.6 11.1 %conditional.4 = ((f32[4,4,256]{2,1,0:T(4,128)S(1)}, f32[4,4,256]{2,1,0:T(4,128)S(1)}, f32[4,4,256,128]{3,2,1,0:T(8,128)})) conditional(s32[]{:T(128)} %convert_element_type.38, (f32[4,4,256]{2,1,0:T(4,128)S(1)}, f32[4,4,256]{2,1,0:T(4,128)S(1)}, f32[4,4,256,128]{3,2,1,0:T(8,128)}) %tuple.85, (pred[256,512]{0,1:T(8,128)(4,1)S(1)}, ...), branch_computations={%region_3.3_spmd, %region_4.6_spmd} | conditional | flops 1098915840 | bytes 54526076 | solution.py:77
  236.3 1.9 fusion.6
  240.1 3.3 %multiply_add_fusion = f32[4,4,256,128]{3,2,1,0:T(8,128)S(1)} fusion(f32[4,4,256,128]{3,2,1,0:T(8,128)S(1)} %copy-done, bf16[512,4,128,1]{0,2,3,1:T(8,128)(2,1)S(1)} %bitcast.89, f32[4,512,256,4]{2,1,3,0:T(8,128)S(1)} %get-tuple-element.543, f32[4,4,256]{2,1,0:T(4,128)S(1)} %max.5, pred[4,256,512]{1,2,0:T(8,128)(4,1)S(1)} %and_or_fusion, ...), kind=kOutput, calls=%fused_computation.16 | convolution fusion | flops 546308096 | bytes 13664256 | tf_op jit(solution)/shard_map/while/body/eval_jaxpr/cond/branch_1_fun/gjqk,kgd->gjqd/dot_general | solution.py:64
  248.5 11.1 %conditional.4 = ((f32[4,4,256]{2,1,0:T(4,128)S(1)}, f32[4,4,256]{2,1,0:T(4,128)S(1)}, f32[4,4,256,128]{3,2,1,0:T(8,128)})) conditional(s32[]{:T(128)} %convert_element_type.38, (f32[4,4,256]{2,1,0:T(4,128)S(1)}, f32[4,4,256]{2,1,0:T(4,128)S(1)}, f32[4,4,256,128]{3,2,1,0:T(8,128)}) %tuple.85, (pred[256,512]{0,1:T(8,128)(4,1)S(1)}, ...), branch_computations={%region_3.3_spmd, %region_4.6_spmd} | conditional | flops 1098915840 | bytes 54526076 | solution.py:77
  251.1 1.9 fusion.6
  254.9 3.3 %multiply_add_fusion = f32[4,4,256,128]{3,2,1,0:T(8,128)S(1)} fusion(f32[4,4,256,128]{3,2,1,0:T(8,128)S(1)} %copy-done, bf16[512,4,128,1]{0,2,3,1:T(8,128)(2,1)S(1)} %bitcast.89, f32[4,512,256,4]{2,1,3,0:T(8,128)S(1)} %get-tuple-element.543, f32[4,4,256]{2,1,0:T(4,128)S(1)} %max.5, pred[4,256,512]{1,2,0:T(8,128)(4,1)S(1)} %and_or_fusion, ...), kind=kOutput, calls=%fused_computation.16 | convolution fusion | flops 546308096 | bytes 13664256 | tf_op jit(solution)/shard_map/while/body/eval_jaxpr/cond/branch_1_fun/gjqk,kgd->gjqd/dot_general | solution.py:64
  259.6 1.9 fusion.24
  (230 shorter events, 103.4 us)
Async XLA Ops:
  6.5 126.4 %all-gather.2.cloned.1.call-start = ((), (), s32[]{:S(2)}) async-start(), calls=%async_computation.2 | async-start | bytes 4456448 | tf_op jit(solution)/shard_map/all_gather | solution.py:82
  23.0 11.4 %collective-permute-start = (bf16[256,512]{1,0:T(8,128)(2,1)S(1)}, bf16[256,512]{1,0:T(8,128)(2,1)S(1)}, u32[]{:S(2)}, u32[]{:S(2)}) collective-permute-start(bf16[256,512]{1,0:T(8,128)(2,1)S(1)} %bitcast.95), channel_id=1, source_target_pairs={{0,2},{2,4},{4,6},{6,8},{8,10},{10,12},{12,14},{14,16},{16,18},{18... | collective-permute-start | bytes 786440 | tf_op jit(solution)/shard_map/ppermute | solution.py:89
  34.3 8.5 %collective-permute-start.1 = (bf16[256,512]{1,0:T(8,128)(2,1)S(1)}, bf16[256,512]{1,0:T(8,128)(2,1)S(1)}, u32[]{:S(2)}, u32[]{:S(2)}) collective-permute-start(bf16[256,512]{1,0:T(8,128)(2,1)S(1)} %collective-permute-done), channel_id=1, source_target_pairs={{0,2},{2,4},{4,6},{6,8},{8,10},{10,12},{12,14},{14,16},{16,18},{18... | collective-permute-start | bytes 786440 | tf_op jit(solution)/shard_map/ppermute | solution.py:89
  39.5 9.9 %collective-permute-start.8 = (bf16[256,512]{1,0:T(8,128)(2,1)S(1)}, bf16[256,512]{1,0:T(8,128)(2,1)S(1)}, u32[]{:S(2)}, u32[]{:S(2)}) collective-permute-start(bf16[256,512]{1,0:T(8,128)(2,1)S(1)} %bitcast.96), channel_id=1, source_target_pairs={{2,0},{4,2},{6,4},{8,6},{10,8},{12,10},{14,12},{16,14},{18,16},{20... | collective-permute-start | bytes 786440 | tf_op jit(solution)/shard_map/ppermute | solution.py:91
  42.8 14.1 %collective-permute-start.2 = (bf16[256,512]{1,0:T(8,128)(2,1)S(1)}, bf16[256,512]{1,0:T(8,128)(2,1)S(1)}, u32[]{:S(2)}, u32[]{:S(2)}) collective-permute-start(bf16[256,512]{1,0:T(8,128)(2,1)S(1)} %collective-permute-done.1), channel_id=1, source_target_pairs={{0,2},{2,4},{4,6},{6,8},{8,10},{10,12},{12,14},{14,16},{16,18},{18... | collective-permute-start | bytes 786440 | tf_op jit(solution)/shard_map/ppermute | solution.py:89
  49.4 12.7 %collective-permute-start.9 = (bf16[256,512]{1,0:T(8,128)(2,1)S(1)}, bf16[256,512]{1,0:T(8,128)(2,1)S(1)}, u32[]{:S(2)}, u32[]{:S(2)}) collective-permute-start(bf16[256,512]{1,0:T(8,128)(2,1)S(1)} %collective-permute-done.8), channel_id=1, source_target_pairs={{2,0},{4,2},{6,4},{8,6},{10,8},{12,10},{14,12},{16,14},{18,16},{20... | collective-permute-start | bytes 786440 | tf_op jit(solution)/shard_map/ppermute | solution.py:91
  56.9 43.8 %copy-start.2 = (bf16[256,512]{1,0:T(8,128)(2,1)}, bf16[256,512]{1,0:T(8,128)(2,1)S(1)}, u32[]{:S(2)}) copy-start(bf16[256,512]{1,0:T(8,128)(2,1)S(1)} %collective-permute-done.2) | copy-start | bytes 786436
  56.9 9.9 %collective-permute-start.3 = (bf16[256,512]{1,0:T(8,128)(2,1)S(1)}, bf16[256,512]{1,0:T(8,128)(2,1)S(1)}, u32[]{:S(2)}, u32[]{:S(2)}) collective-permute-start(bf16[256,512]{1,0:T(8,128)(2,1)S(1)} %collective-permute-done.2), channel_id=1, source_target_pairs={{0,2},{2,4},{4,6},{6,8},{8,10},{10,12},{12,14},{14,16},{16,18},{18... | collective-permute-start | bytes 786440 | tf_op jit(solution)/shard_map/ppermute | solution.py:89
  62.1 12.2 %collective-permute-start.10 = (bf16[256,512]{1,0:T(8,128)(2,1)S(1)}, bf16[256,512]{1,0:T(8,128)(2,1)S(1)}, u32[]{:S(2)}, u32[]{:S(2)}) collective-permute-start(bf16[256,512]{1,0:T(8,128)(2,1)S(1)} %collective-permute-done.9), channel_id=1, source_target_pairs={{2,0},{4,2},{6,4},{8,6},{10,8},{12,10},{14,12},{16,14},{18,16},{20... | collective-permute-start | bytes 786440 | tf_op jit(solution)/shard_map/ppermute | solution.py:91
  66.9 33.9 %copy-start.7 = (bf16[256,512]{1,0:T(8,128)(2,1)}, bf16[256,512]{1,0:T(8,128)(2,1)S(1)}, u32[]{:S(2)}) copy-start(bf16[256,512]{1,0:T(8,128)(2,1)S(1)} %collective-permute-done.3) | copy-start | bytes 786436
  66.9 9.2 %collective-permute-start.4 = (bf16[256,512]{1,0:T(8,128)(2,1)S(1)}, bf16[256,512]{1,0:T(8,128)(2,1)S(1)}, u32[]{:S(2)}, u32[]{:S(2)}) collective-permute-start(bf16[256,512]{1,0:T(8,128)(2,1)S(1)} %collective-permute-done.3), channel_id=1, source_target_pairs={{0,2},{2,4},{4,6},{6,8},{8,10},{10,12},{12,14},{14,16},{16,18},{18... | collective-permute-start | bytes 786440 | tf_op jit(solution)/shard_map/ppermute | solution.py:89
  74.3 26.5 %copy-start.3 = (bf16[256,512]{1,0:T(8,128)(2,1)}, bf16[256,512]{1,0:T(8,128)(2,1)S(1)}, u32[]{:S(2)}) copy-start(bf16[256,512]{1,0:T(8,128)(2,1)S(1)} %collective-permute-done.10) | copy-start | bytes 786436
  74.3 8.6 %collective-permute-start.11 = (bf16[256,512]{1,0:T(8,128)(2,1)S(1)}, bf16[256,512]{1,0:T(8,128)(2,1)S(1)}, u32[]{:S(2)}, u32[]{:S(2)}) collective-permute-start(bf16[256,512]{1,0:T(8,128)(2,1)S(1)} %collective-permute-done.10), channel_id=1, source_target_pairs={{2,0},{4,2},{6,4},{8,6},{10,8},{12,10},{14,12},{16,14},{18,16},{20... | collective-permute-start | bytes 786440 | tf_op jit(solution)/shard_map/ppermute | solution.py:91
  76.0 15.6 %copy-start.8 = (bf16[256,512]{1,0:T(8,128)(2,1)}, bf16[256,512]{1,0:T(8,128)(2,1)S(1)}, u32[]{:S(2)}) copy-start(bf16[256,512]{1,0:T(8,128)(2,1)S(1)} %collective-permute-done.4) | copy-start | bytes 786436
  76.0 8.6 %collective-permute-start.5 = (bf16[256,512]{1,0:T(8,128)(2,1)S(1)}, bf16[256,512]{1,0:T(8,128)(2,1)S(1)}, u32[]{:S(2)}, u32[]{:S(2)}) collective-permute-start(bf16[256,512]{1,0:T(8,128)(2,1)S(1)} %collective-permute-done.4), channel_id=1, source_target_pairs={{0,2},{2,4},{4,6},{6,8},{8,10},{10,12},{12,14},{14,16},{16,18},{18... | collective-permute-start | bytes 786440 | tf_op jit(solution)/shard_map/ppermute | solution.py:89
  82.9 17.9 %copy-start.5 = (bf16[256,512]{1,0:T(8,128)(2,1)}, bf16[256,512]{1,0:T(8,128)(2,1)S(1)}, u32[]{:S(2)}) copy-start(bf16[256,512]{1,0:T(8,128)(2,1)S(1)} %collective-permute-done.11) | copy-start | bytes 786436
  82.9 8.7 %collective-permute-start.12 = (bf16[256,512]{1,0:T(8,128)(2,1)S(1)}, bf16[256,512]{1,0:T(8,128)(2,1)}, u32[]{:S(2)}, u32[]{:S(2)}) collective-permute-start(bf16[256,512]{1,0:T(8,128)(2,1)S(1)} %collective-permute-done.11), channel_id=1, source_target_pairs={{2,0},{4,2},{6,4},{8,6},{10,8},{12,10},{14,12},{16,14},{18,16},{20... | collective-permute-start | bytes 786440 | tf_op jit(solution)/shard_map/ppermute | solution.py:91
  84.6 7.0 %copy-start.9 = (bf16[256,512]{1,0:T(8,128)(2,1)}, bf16[256,512]{1,0:T(8,128)(2,1)S(1)}, u32[]{:S(2)}) copy-start(bf16[256,512]{1,0:T(8,128)(2,1)S(1)} %collective-permute-done.5) | copy-start | bytes 786436
  84.6 8.6 %collective-permute-start.6 = (bf16[256,512]{1,0:T(8,128)(2,1)S(1)}, bf16[256,512]{1,0:T(8,128)(2,1)}, u32[]{:S(2)}, u32[]{:S(2)}) collective-permute-start(bf16[256,512]{1,0:T(8,128)(2,1)S(1)} %collective-permute-done.5), channel_id=1, source_target_pairs={{0,2},{2,4},{4,6},{6,8},{8,10},{10,12},{12,14},{14,16},{16,18},{18... | collective-permute-start | bytes 786440 | tf_op jit(solution)/shard_map/ppermute | solution.py:89
  91.6 9.9 %collective-permute-start.13 = (bf16[256,512]{1,0:T(8,128)(2,1)}, bf16[256,512]{1,0:T(8,128)(2,1)}, u32[]{:S(2)}, u32[]{:S(2)}) collective-permute-start(bf16[256,512]{1,0:T(8,128)(2,1)} %collective-permute-done.12), channel_id=1, source_target_pairs={{2,0},{4,2},{6,4},{8,6},{10,8},{12,10},{14,12},{16,14},{18,16},{20... | collective-permute-start | bytes 786440 | tf_op jit(solution)/shard_map/ppermute | solution.py:91
  93.2 8.9 %collective-permute-start.7 = (bf16[256,512]{1,0:T(8,128)(2,1)}, bf16[256,512]{1,0:T(8,128)(2,1)}, u32[]{:S(2)}, u32[]{:S(2)}) collective-permute-start(bf16[256,512]{1,0:T(8,128)(2,1)} %collective-permute-done.6), channel_id=1, source_target_pairs={{0,2},{2,4},{4,6},{6,8},{8,10},{10,12},{12,14},{14,16},{16,18},{18... | collective-permute-start | bytes 786440 | tf_op jit(solution)/shard_map/ppermute | solution.py:89
  101.5 14.3 %copy-start.4 = (bf16[256,512]{1,0:T(8,128)(2,1)S(1)}, bf16[256,512]{1,0:T(8,128)(2,1)}, u32[]{:S(2)}) copy-start(bf16[256,512]{1,0:T(8,128)(2,1)} %copy-done.3) | copy-start | bytes 786436
  101.5 15.0 %copy-start.6 = (bf16[256,512]{1,0:T(8,128)(2,1)S(1)}, bf16[256,512]{1,0:T(8,128)(2,1)}, u32[]{:S(2)}) copy-start(bf16[256,512]{1,0:T(8,128)(2,1)} %copy-done.5) | copy-start | bytes 786436
  101.6 19.1 %collective-permute-start.14 = (bf16[256,512]{1,0:T(8,128)(2,1)}, bf16[256,512]{1,0:T(8,128)(2,1)S(1)}, u32[]{:S(2)}, u32[]{:S(2)}) collective-permute-start(bf16[256,512]{1,0:T(8,128)(2,1)} %collective-permute-done.13), channel_id=1, source_target_pairs={{2,0},{4,2},{6,4},{8,6},{10,8},{12,10},{14,12},{16,14},{18,16},{20... | collective-permute-start | bytes 786440 | tf_op jit(solution)/shard_map/ppermute | solution.py:91
  149.2 1.9 copy-start
  154.4 1.3 copy-start.1
  164.0 1.9 copy-start
  169.2 1.3 copy-start.1
  178.8 1.9 copy-start
  184.1 1.3 copy-start.1
  193.7 1.9 copy-start
  198.9 1.3 copy-start.1
  208.5 1.9 copy-start
  213.7 1.3 copy-start.1
  223.4 1.9 copy-start
  228.6 1.3 copy-start.1
  238.2 1.9 copy-start
  243.4 1.3 copy-start.1
  253.0 1.9 copy-start
  258.2 1.3 copy-start.1
Sparse Core Ops, SparseCore 0:
  15.4 62.5 all-gather.1
